TPU v7x, 512 devices: a whole 4x8x8 slice. The times are simulated.
512 devices in a mesh: dp: 16 (over y, core), table: 32 (over x, z).
Axes of the slice: x: 4, y: 8, z: 8, core: 2. Of those that a mesh axis runs over, the one named last changes fastest.
Arguments:
- embedded: bfloat16 [2, 32768, 4096], P(None, 'dp', 'table'), may hold values from -1.1953125 to 1.1953125
- resid_grad: bfloat16 [2, 32768, 4096], P(None, 'dp', 'table'), may hold values from -0.29882812 to 0.29882812
- query_grad: bfloat16 [2, 32768, 2048], P(None, ('dp', 'table')), may hold values from -0.59765625 to 0.59765625
- query_weight: bfloat16 [4096, 2048], P('table'), may hold values from -0.09375 to 0.09375
- ngram_rows: int32 [2, 32768, 4], P(None, 'dp'), may hold values from 0 to 3199999, as said below
- touched_rows: int32 [32, 4, 12], replicated, may hold values from -1 to 3199999, as said below
- row_values: float32 [32, 4, 12, 1024], P('table'), may hold values from -6 to 6
- row_mean: float32 [32, 4, 12, 1024], P('table'), may hold values from -0.6 to 0.6
- row_square: float32 [32, 4, 12, 1024], P('table'), may hold values from 0.01 to 0.1
Outputs:
- weight_grad: float32 [4096, 2048], P('table')
- new_values: float32 [32, 4, 12, 1024], P('table')
- new_mean: float32 [32, 4, 12, 1024], P('table')
- new_square: float32 [32, 4, 12, 1024], P('table')
Inputs may be any that keep to these rules, and one draw needn't show every extreme that they name: `touched_rows`: owner o's list for slice s holds 1 to 12 distinct row ids of [o * 100000, (o + 1) * 100000) first, then -1; in every slice some owner's list is full. `ngram_rows`: every id of slice s is one of the listed rows of owner id // 100000 for slice s.
All inputs are finite; a program needn't handle non-finite values.
Results may differ from a plain program's by a relative error of at most 0.0003.
Values may be sent and summed in bfloat16 or wider, within the bound.
No kernel may reach another device: no remote copies, remote signals or barrier semaphores. Data moves between devices by JAX's collectives and lax.ppermute only.
A program may use at most 64 MiB of HBM per device.

v0:
```python
import jax
import jax.numpy as jnp
from jax import lax
from jax.sharding import PartitionSpec as P

SLICES = 4
SW = 1024


beta_one = 0.9
beta_two = 0.95
learn_rate = 0.01
adam_eps = 1e-08
adam_step = 10


def adam_rows(grads, values, mean, square, live):
    corr_one = 1.0 - beta_one**adam_step
    corr_two = 1.0 - beta_two**adam_step
    mean_next = beta_one * mean + (1.0 - beta_one) * grads
    square_next = beta_two * square + (1.0 - beta_two) * grads * grads
    update = learn_rate * (mean_next / corr_one) / (jnp.sqrt(square_next / corr_two) + adam_eps)
    values_next = values - update
    return (
        jnp.where(live, values_next, values),
        jnp.where(live, mean_next, mean),
        jnp.where(live, square_next, square),
    )


def make_step(emb_part, weight_part, carry, piece):
    back_part, wgrad = carry
    back = jnp.einsum("mrh,ph->mrp", piece, weight_part, preferred_element_type=jnp.float32)
    back_part = back
    wgrad = wgrad + jnp.einsum("mrp,mrh->ph", emb_part, piece, preferred_element_type=jnp.float32)
    return (back_part, wgrad)


def local(
    embedded,
    resid_grad,
    query_grad,
    query_weight,
    ngram_rows,
    touched_rows,
    row_values,
    row_mean,
    row_square,
):
    micro_count, group_tokens, width_part = embedded.shape
    hidden = query_grad.shape[2]
    tables = lax.axis_size("table")
    table_idx = lax.axis_index("table")
    zero_grad = jnp.zeros((width_part, hidden), jnp.float32)
    wgrad = zero_grad
    backs = []
    for micro in range(micro_count):
        start_back = jnp.zeros((1, group_tokens, width_part), jnp.float32)
        back_one, wgrad = make_step(
            embedded[micro : micro + 1],
            query_weight,
            (start_back, wgrad),
            lax.all_gather(query_grad[micro : micro + 1], "table", axis=1, tiled=True),
        )
        backs.append(back_one)
    back_all = jnp.concatenate(backs, axis=0)
    emb_grad = resid_grad.astype(jnp.float32) + back_all
    weight_grad = lax.psum(wgrad, "dp")
    slice_idx = table_idx * width_part // SW
    ids = lax.dynamic_index_in_dim(ngram_rows, slice_idx, 2, False)
    listed = lax.dynamic_index_in_dim(touched_rows, slice_idx, 1, False)
    entries = listed.shape[1]
    flat_list = listed.reshape(tables * entries)
    onehot = (ids[:, :, None] == flat_list[None, None, :]).astype(jnp.float32)
    buckets = jnp.einsum(
        "mtk,mtp->kp",
        onehot,
        emb_grad,
        precision=lax.Precision.HIGHEST,
        preferred_element_type=jnp.float32,
    )
    buckets = buckets.reshape(tables, entries, width_part)
    arrived = lax.all_to_all(buckets, "table", split_axis=0, concat_axis=0, tiled=True)
    per_slice = tables // SLICES
    local_grad = (
        arrived.reshape(SLICES, per_slice, entries, width_part)
        .transpose(0, 2, 1, 3)
        .reshape(SLICES, entries, per_slice * width_part)
    )
    mine = lax.dynamic_index_in_dim(touched_rows, table_idx, 0, False)
    live = (mine >= 0)[..., None]
    values = row_values[0]
    mean = row_mean[0]
    square = row_square[0]
    grads = lax.psum(local_grad, "dp")
    values_next, mean_next, square_next = adam_rows(grads, values, mean, square, live)
    return (weight_grad, values_next[None], mean_next[None], square_next[None])


def solution(mesh):
    placed = (
        P(None, "dp", "table"),
        P(None, "dp", "table"),
        P(None, ("dp", "table"), None),
        P("table", None),
        P(None, "dp", None),
        P(),
        P("table", None, None, None),
        P("table", None, None, None),
        P("table", None, None, None),
    )
    return jax.shard_map(
        local,
        mesh=mesh,
        in_specs=placed,
        out_specs=(
            P("table", None),
            P("table", None, None, None),
            P("table", None, None, None),
            P("table", None, None, None),
        ),
        check_vma=False,
    )
```

profile of v0, /device:TPU:1, one launch (start us, length us, event | category | flops | bytes accessed | tf_op | source)
XLA Modules:
  0.0 381.2 jit_solution(2230396503521548309)
XLA Ops:
  7.2 0.0 copy-start
  7.2 0.0 all-gather.5.cloned.1.call-start
  7.2 1.9 fusion.37
  9.1 0.0 all-gather.5.cloned.1.call-update
  9.2 0.0 all-gather.3.cloned.1.call-start
  9.2 0.7 all-gather.3.cloned.1.call-update
  9.9 0.9 constant_dynamic-slice_fusion.1
  10.8 0.8 constant_dynamic-slice_fusion
  11.6 0.1 copy.22
  11.7 0.1 eq.19
  11.8 108.8 %all-gather.5.cloned.1.call-done = bf16[1,2048,2048]{2,1,0:T(8,128)(2,1)} async-done(((bf16[1,64,2048]{2,1,0:T(8,128)(2,1)}), bf16[1,2048,2048]{2,1,0:T(8,128)(2,1)}) %all-gather.5.cloned.1.call-update) | async-done | bytes 8388624 | tf_op jit(solution)/shard_map/all_gather | solution.py:63
  120.6 0.0 copy-done
  120.6 6.7 %fusion.15 = f32[1,2048,128]{2,1,0:T(8,128)} fusion(bf16[128,2048]{1,0:T(8,128)(2,1)S(1)} %copy-done, bf16[1,2048,2048]{2,1,0:T(8,128)(2,1)} %all-gather.5.cloned.1.call-done), kind=kOutput, calls=%fused_computation.13 | convolution fusion | flops 1073741824 | bytes 9961472 | tf_op jit(solution)/shard_map/mrh,ph->mrp/dot_general | solution.py:33
  127.3 0.0 copy-start.6
  127.3 0.0 copy-start.1
  127.3 97.1 %all-gather.3.cloned.1.call-done = bf16[1,2048,2048]{2,1,0:T(8,128)(2,1)} async-done(((bf16[1,64,2048]{2,1,0:T(8,128)(2,1)}), bf16[1,2048,2048]{2,1,0:T(8,128)(2,1)}) %all-gather.3.cloned.1.call-update) | async-done | bytes 8388624 | tf_op jit(solution)/shard_map/all_gather | solution.py:63
  224.4 0.0 copy-start.7
  224.4 5.8 %fusion.12 = f32[1,2048,128]{2,1,0:T(8,128)S(1)} fusion(bf16[128,2048]{1,0:T(8,128)(2,1)S(1)} %copy-done, bf16[1,2048,2048]{2,1,0:T(8,128)(2,1)} %all-gather.3.cloned.1.call-done), kind=kOutput, calls=%fused_computation.12 | convolution fusion | flops 1073741824 | bytes 9961472 | tf_op jit(solution)/shard_map/mrh,ph->mrp/dot_general | solution.py:33
  230.2 0.0 copy-done.6
  230.2 0.0 copy-done.7
  230.2 3.1 fusion.24
  233.3 0.7 reshape.46
  234.1 5.2 %all-to-all-start = ((f32[32,12,128]{2,1,0:T(8,128)}), f32[32,12,128]{2,1,0:T(8,128)S(1)}, u32[]{:S(2)}, u32[]{:S(2)}) async-start(f32[32,12,128]{2,1,0:T(8,128)} %reshape.46), calls=%async_computation | async-start | bytes 524288 | tf_op jit(solution)/shard_map/all_to_all | solution.py:83
  239.2 0.2 all-reduce.3.cloned.1.call-start
  239.5 0.0 copy-done.1
  239.5 4.7 %fusion.2 = f32[128,2048]{1,0:T(8,128)S(1)} fusion(bf16[1,2048,2048]{2,1,0:T(8,128)(2,1)} %all-gather.5.cloned.1.call-done, bf16[2,2048,128]{2,1,0:T(8,128)(2,1)S(1)} %copy-done.1), kind=kOutput, calls=%fused_computation.2 | convolution fusion | flops 1073741824 | bytes 9961472 | tf_op jit(solution)/shard_map/mrp,mrh->ph/dot_general | solution.py:35
  244.1 0.0 copy-start.5
  244.1 0.0 copy-start.2
  244.2 0.0 copy-start.3
  244.2 0.0 copy-start.4
  244.2 5.7 %fusion.18 = f32[128,2048]{1,0:T(8,128)} fusion(f32[128,2048]{1,0:T(8,128)S(1)} %fusion.2, bf16[1,2048,2048]{2,1,0:T(8,128)(2,1)} %all-gather.3.cloned.1.call-done, bf16[2,2048,128]{2,1,0:T(8,128)(2,1)S(1)} %copy-done.1), kind=kOutput, calls=%fused_computation.14 | convolution fusion | flops 1074003968 | bytes 11010048 | tf_op jit(solution)/shard_map/mrp,mrh->ph/dot_general | solution.py:35
  249.9 0.0 all-to-all-done
  249.9 0.1 copy.23
  249.9 0.7 reshape.48
  250.7 0.0 all-reduce.3.cloned.1.call-update
  250.7 0.0 copy-done.5
  250.7 0.1 constant_dynamic-slice_fusion.2
  250.8 0.1 copy.25
  250.9 0.1 copy.21
  251.0 119.2 %all-reduce.3.cloned.1.call-done = (f32[128,2048]{1,0:T(8,128)}, f32[4,12,1024]{2,0,1:T(4,128)}) async-done(((f32[128,2048]{1,0:T(8,128)}, f32[4,12,1024]{2,0,1:T(4,128)}), (f32[128,2048]{1,0:T(8,128)}, f32[4,12,1024]{2,0,1:T(4,128)})) %all-reduce.3.cloned.1.call-update) | async-done | bytes 1245200 | tf_op jit(solution)/shard_map/psum | solution.py:68
  370.2 0.0 copy-done.2
  370.2 0.0 copy-done.3
  370.2 0.0 copy-done.4
  370.2 2.1 fusion.33
  372.4 2.3 copy.30
  (2 shorter events, 0.0 us)
Async XLA Ops:
  7.2 113.4 %copy-start = (bf16[128,2048]{1,0:T(8,128)(2,1)S(1)}, bf16[128,2048]{1,0:T(8,128)(2,1)}, u32[]{:S(2)}) copy-start(bf16[128,2048]{1,0:T(8,128)(2,1)} %param.12) | copy-start | bytes 1572868
  7.2 113.4 %all-gather.5.cloned.1.call-start = ((), (), s32[]{:S(2)}) async-start(), calls=%async_computation.2 | async-start | bytes 8650752 | tf_op jit(solution)/shard_map/all_gather | solution.py:63
  9.2 215.2 %all-gather.3.cloned.1.call-start = ((), (), s32[]{:S(2)}) async-start(), calls=%async_computation.1 | async-start | bytes 8650752 | tf_op jit(solution)/shard_map/all_gather | solution.py:63
  127.3 103.0 %copy-start.6 = (bf16[2,2048,128]{2,1,0:T(8,128)(2,1)S(1)}, bf16[2,2048,128]{2,1,0:T(8,128)(2,1)}, u32[]{:S(2)}) copy-start(bf16[2,2048,128]{2,1,0:T(8,128)(2,1)} %param.10) | copy-start | bytes 3145732
  127.3 112.2 %copy-start.1 = (bf16[2,2048,128]{2,1,0:T(8,128)(2,1)S(1)}, bf16[2,2048,128]{2,1,0:T(8,128)(2,1)}, u32[]{:S(2)}) copy-start(bf16[2,2048,128]{2,1,0:T(8,128)(2,1)} %param.9) | copy-start | bytes 3145732
  224.4 5.9 %copy-start.7 = (f32[1,2048,128]{2,1,0:T(8,128)S(1)}, f32[1,2048,128]{2,1,0:T(8,128)}, u32[]{:S(2)}) copy-start(f32[1,2048,128]{2,1,0:T(8,128)} %fusion.15) | copy-start | bytes 3145732
  234.1 15.8 %all-to-all-start = ((f32[32,12,128]{2,1,0:T(8,128)}), f32[32,12,128]{2,1,0:T(8,128)S(1)}, u32[]{:S(2)}, u32[]{:S(2)}) async-start(f32[32,12,128]{2,1,0:T(8,128)} %reshape.46), calls=%async_computation | async-start | bytes 524288 | tf_op jit(solution)/shard_map/all_to_all | solution.py:83
  239.2 131.0 %all-reduce.3.cloned.1.call-start = ((), (), s32[]{:S(2)}) async-start(), calls=%async_computation.3 | async-start | bytes 2490368 | tf_op jit(solution)/shard_map/psum | solution.py:68
  244.1 6.6 %copy-start.5 = (s32[32,4,12]{0,1,2:T(4,128)S(1)}, s32[32,4,12]{0,1,2:T(4,128)}, u32[]{:S(2)}) copy-start(s32[32,4,12]{0,1,2:T(4,128)} %param.14) | copy-start | bytes 18436
  244.1 126.1 %copy-start.2 = (f32[1,4,12,1024]{3,1,2,0:T(4,128)S(1)}, f32[1,4,12,1024]{3,1,2,0:T(4,128)}, u32[]{:S(2)}) copy-start(f32[1,4,12,1024]{3,1,2,0:T(4,128)} %param.17) | copy-start | bytes 589828
  244.2 126.1 %copy-start.3 = (f32[1,4,12,1024]{3,1,2,0:T(4,128)S(1)}, f32[1,4,12,1024]{3,1,2,0:T(4,128)}, u32[]{:S(2)}) copy-start(f32[1,4,12,1024]{3,1,2,0:T(4,128)} %param.16) | copy-start | bytes 589828
  244.2 126.0 %copy-start.4 = (f32[1,4,12,1024]{3,1,2,0:T(4,128)S(1)}, f32[1,4,12,1024]{3,1,2,0:T(4,128)}, u32[]{:S(2)}) copy-start(f32[1,4,12,1024]{3,1,2,0:T(4,128)} %param.15) | copy-start | bytes 589828
Sparse Core Ops, SparseCore 0:
  11.7 108.7 all-gather.4
  123.7 100.5 all-gather.2
  250.8 119.3 all-reduce.2
where the time goes:
time: 382 us; the launch traced here: 381 us
  waiting for transfers between devices  326 us (85%)
  matrix products  26 us (7%)
  between operations  13.9 us (4%)
  local copies, waits for them, and re-layouts  7.9 us (2%)
  starting transfers between devices  5.47 us (1%)
    all_gather x2, waiting for transfers between devices, local(): lax.all_gather(query_grad[micro:micro + 1], 'table', axis=1, tiled=True)  206 us
    psum x1, waiting for transfers between devices, local(): weight_grad = lax.psum(wgrad, 'dp')  119 us
    dot_general x2, matrix products, make_step(): jnp.einsum('mrh,ph->mrp', piece, weight_part, preferred_element_type=jnp....  12.6 us
    dot_general x2, matrix products, make_step(): jnp.einsum('mrp,mrh->ph', emb_part, piece, preferred_element_type=jnp.flo...  10.4 us
  transfers between devices with their start and end apart: 4, of which 3 were waited for; matrix products, arithmetic and copies ran while one was open for 5% of the time, Pallas kernels for 0%

commit v1 on v0

v1 whole, which is shorter than its diff:
```python
import jax
import jax.numpy as jnp
from jax import lax
from jax.sharding import Mesh, PartitionSpec as P

SW = 1024

beta_one = 0.9
beta_two = 0.95
learn_rate = 0.01
adam_eps = 1e-08
adam_step = 10

f32 = jnp.float32
bf16 = jnp.bfloat16


def adam_rows(grads, values, mean, square, live):
    corr_one = 1.0 - beta_one**adam_step
    corr_two = 1.0 - beta_two**adam_step
    mean_next = beta_one * mean + (1.0 - beta_one) * grads
    square_next = beta_two * square + (1.0 - beta_two) * grads * grads
    update = learn_rate * (mean_next / corr_one) / (jnp.sqrt(square_next / corr_two) + adam_eps)
    values_next = values - update
    return (
        jnp.where(live, values_next, values),
        jnp.where(live, mean_next, mean),
        jnp.where(live, square_next, square),
    )


def over_tokens(left, right):
    return lax.dot_general(left, right, (((0,), (0,)), ((), ())), preferred_element_type=f32)


def shift(array, axis, step):
    size = lax.axis_size(axis)
    return lax.ppermute(array, axis, [(i, (i + step) % size) for i in range(size)])


def local(
    embedded,
    resid_grad,
    query_grad,
    query_weight,
    ngram_rows,
    touched_rows,
    row_values,
    row_mean,
    row_square,
):
    micro, group, width = embedded.shape
    per, hidden = query_grad.shape[1:]
    nx, nz, ny = lax.axis_size("x"), lax.axis_size("z"), lax.axis_size("y")
    x_idx, z_idx, core = lax.axis_index("x"), lax.axis_index("z"), lax.axis_index("core")
    tables, slices, entries = touched_rows.shape
    part = hidden // nx
    tokens = micro * group
    groups = ny * 2
    rows_p = width // groups

    def token_order(array):
        tail = array.shape[2:]
        array = array.reshape((micro, nx, nz, per) + tail)
        return array.transpose((2, 1, 0, 3) + tuple(range(4, array.ndim))).reshape((tokens,) + tail)

    def by_part(array):
        return array.reshape(-1, nx, part).transpose(1, 0, 2)

    query = lax.all_to_all(by_part(query_grad), "x", 0, 0, tiled=True)
    query = lax.all_gather(query.reshape(nx * micro * per, part), "z", axis=0, tiled=True)

    weight = lax.all_to_all(by_part(query_weight), "x", 0, 0, tiled=True)

    emb = token_order(embedded)
    half = tokens // 2
    emb_back = shift(emb, "x", 1)
    emb_front = shift(emb, "x", -1)
    far_low = shift(emb_back[:half], "x", 1)
    far_high = shift(emb_front[half:], "x", -1)
    emb_far = jnp.concatenate([far_low, far_high], axis=0)
    emb_all = [emb, emb_front, emb_far, emb_back]

    ids = token_order(ngram_rows)
    lists = touched_rows.transpose(1, 2, 0).reshape(slices, entries * tables)

    def onehot(ids_of, list_of):
        return (ids_of[:, None] == list_of[None, :]).astype(bf16)

    own_ids = lax.dynamic_index_in_dim(ids, x_idx, 1, False)
    own_list = lax.dynamic_index_in_dim(lists, x_idx, 0, False)
    resid_rows = over_tokens(onehot(own_ids, own_list), token_order(resid_grad))

    row_parts = []
    for s in range(slices):
        seg = over_tokens(onehot(ids[:, s], lists[s]), query)
        high = lax.reduce_precision(seg, 8, 7)
        low = (seg - high).astype(bf16)
        one = lax.dot_general(high.astype(bf16), weight[s], (((1,), (1,)), ((), ())), preferred_element_type=f32)
        two = lax.dot_general(low, weight[s], (((1,), (1,)), ((), ())), preferred_element_type=f32)
        row_parts.append(one + two + jnp.where(x_idx == s, resid_rows, 0.0))
    row_sum = jnp.stack(row_parts).reshape(groups, slices * entries // groups * tables, width)

    w_parts = [over_tokens(piece, query) for piece in emb_all]
    w_sum = jnp.stack(w_parts)
    lanes = 128
    w_sum = w_sum.reshape(nx, groups, rows_p, part // lanes, lanes).transpose(1, 0, 3, 2, 4)
    w_sum = w_sum.reshape(groups, nx * part // lanes * rows_p, lanes)
    both = jnp.concatenate([w_sum, row_sum], axis=1)
    both = both.reshape(ny, 2, both.shape[1], lanes)
    first = core == 0
    send = jnp.where(first, both[:, 1], both[:, 0])
    keep = jnp.where(first, both[:, 0], both[:, 1])
    pair = keep + shift(send, "core", 1)
    pieces = lax.all_to_all(pair, "y", 0, 0, tiled=True)
    total = jnp.sum(pieces, axis=0)

    w_rows = nx * part // lanes * rows_p
    w_mine = total[:w_rows].reshape(nx, part // lanes * rows_p, lanes)
    twice = jnp.concatenate([w_mine, w_mine], axis=0)
    w_mine = lax.dynamic_slice_in_dim(twice, nx - x_idx, nx, 0)
    w_mine = lax.all_to_all(w_mine, "x", 0, 0, tiled=True).reshape(w_rows, lanes)

    pairs = slices * entries // groups
    r_mine = total[w_rows:].reshape(pairs, tables, width).transpose(1, 0, 2)
    r_mine = lax.all_to_all(r_mine, ("x", "z"), 0, 0, tiled=True)
    r_mine = jnp.sum(r_mine.reshape(nx, nz, pairs, width), axis=0)
    r_mine = r_mine.transpose(1, 0, 2).reshape(pairs * nz, lanes)

    piece = jnp.concatenate([w_mine, r_mine], axis=0)
    spread = jnp.broadcast_to(piece[None], (ny,) + piece.shape)
    mine = lax.all_to_all(spread, "y", 0, 0, tiled=True)
    other = shift(mine, "core", 1)
    full = jnp.stack([jnp.where(first, mine, other), jnp.where(first, other, mine)], axis=1)
    full = full.reshape((groups,) + piece.shape)
    weight_grad = full[:, :w_rows].reshape(groups, hidden // lanes, rows_p, lanes)
    weight_grad = weight_grad.transpose(0, 2, 1, 3).reshape(width, hidden)
    grads = full[:, w_rows:].reshape(slices, entries, nz * width)

    mine_rows = lax.dynamic_index_in_dim(touched_rows, x_idx * nz + z_idx, 0, False)
    live = (mine_rows >= 0)[..., None]
    values_next, mean_next, square_next = adam_rows(grads, row_values[0], row_mean[0], row_square[0], live)
    return (weight_grad, values_next[None], mean_next[None], square_next[None])


def solution(mesh):
    fine = Mesh(mesh.devices.reshape(8, 2, 4, 8), ("y", "core", "x", "z"))
    dp, table = ("y", "core"), ("x", "z")
    placed = (
        P(None, dp, table),
        P(None, dp, table),
        P(None, dp + table, None),
        P(table, None),
        P(None, dp, None),
        P(),
        P(table, None, None, None),
        P(table, None, None, None),
        P(table, None, None, None),
    )
    return jax.shard_map(
        local,
        mesh=fine,
        in_specs=placed,
        out_specs=(
            P(table, None),
            P(table, None, None, None),
            P(table, None, None, None),
            P(table, None, None, None),
        ),
        check_vma=False,
    )
```

time: 382 us -> 214 us (0.56)
  waiting for transfers between devices: 326 us -> 77.4 us
  starting transfers between devices: 5.47 us -> 42.9 us
  blocking collectives: 0 us -> 30.4 us
  local copies, waits for them, and re-layouts: 7.9 us -> 14.8 us
  matrix products: 26 us -> 30.4 us
    all_gather x2 -> x1, waiting for transfers between devices: 206 us -> 31 us  [local(): lax.all_gather(query.reshape(nx * micro * per, part), 'z', axis=0, tiled=...]
    psum x1 -> x0, waiting for transfers between devices: 119 us -> none  [local(): weight_grad = lax.psum(wgrad, 'dp')]
    all_to_all x1 -> x4, waiting for transfers between devices: 0.01 us -> 39 us  [the longest x1 26.4 us: local(): pieces = lax.all_to_all(pair, 'y', 0, 0, tiled=True)]
    all_to_all x0 -> x2, blocking collectives: none -> 30.4 us  [the longest x1 18.7 us: local(): mine = lax.all_to_all(spread, 'y', 0, 0, tiled=True)]
    ppermute x0 -> x6, starting transfers between devices: none -> 23 us  [shift(): lax.ppermute(array, axis, [(i, (i + step) % size) for i in range(size)])]
    all_to_all x1 -> x4, starting transfers between devices: 5.17 us -> 19.9 us  [the longest x1 6.64 us: local(): r_mine = lax.all_to_all(r_mine, ('x', 'z'), 0, 0, tiled=True)]
    ppermute x0 -> x6, waiting for transfers between devices: none -> 7.41 us  [shift(): lax.ppermute(array, axis, [(i, (i + step) % size) for i in range(size)])]
    dot_general x5 -> x17, matrix products: 26 us -> 30.4 us  [the longest x9 28.3 us: over_tokens(): lax.dot_general(left, right, (((0,), (0,)), ((), ())), preferred_element_...]
  transfers between devices with their start and end apart: 4 -> 11, of which waited for: 3 -> 7; matrix products, arithmetic and copies ran while one was open for 5% -> 13% of each run, Pallas kernels for 0% -> 0%
where the time goes in v1:
time: 214 us; the launch traced here: 213 us
  waiting for transfers between devices  77.4 us (36%)
  starting transfers between devices  42.9 us (20%)
  blocking collectives  30.4 us (14%)
  matrix products  30.4 us (14%)
  local copies, waits for them, and re-layouts  14.8 us (7%)
  between operations  14.5 us (7%)
  other arithmetic  2.73 us (1%)
    all_gather x1, waiting for transfers between devices, local(): lax.all_gather(query.reshape(nx * micro * per, part), 'z', axis=0, tiled=...  31 us
    dot_general x9, matrix products, over_tokens(): lax.dot_general(left, right, (((0,), (0,)), ((), ())), preferred_element_...  28.3 us
    all_to_all x1, waiting for transfers between devices, local(): pieces = lax.all_to_all(pair, 'y', 0, 0, tiled=True)  26.4 us
    ppermute x6, starting transfers between devices, shift(): lax.ppermute(array, axis, [(i, (i + step) % size) for i in range(size)])  23 us
    all_to_all x1, blocking collectives, local(): mine = lax.all_to_all(spread, 'y', 0, 0, tiled=True)  18.7 us
    all_to_all x1, blocking collectives, local(): query = lax.all_to_all(by_part(query_grad), 'x', 0, 0, tiled=True)  11.7 us
    all_to_all x1, waiting for transfers between devices, local(): r_mine = lax.all_to_all(r_mine, ('x', 'z'), 0, 0, tiled=True)  8.21 us
    ppermute x6, waiting for transfers between devices, shift(): lax.ppermute(array, axis, [(i, (i + step) % size) for i in range(size)])  7.41 us
  transfers between devices with their start and end apart: 11, of which 7 were waited for; matrix products, arithmetic and copies ran while one was open for 13% of the time, Pallas kernels for 0%

profile of v1, /device:TPU:1, one launch (start us, length us, event | category | flops | bytes accessed | tf_op | source)
XLA Modules:
  0.0 213.3 jit_solution(14318160484905589885)
XLA Ops:
  7.2 1.5 reshape.141
  8.9 11.7 %all_to_all.30 = bf16[4,128,512]{2,1,0:T(8,128)(2,1)S(1)} all-to-all(bf16[4,128,512]{2,1,0:T(8,128)(2,1)S(1)} %copy.185), channel_id=1, replica_groups=mesh['y'=8,'core'=2,'x'=4,'z'=8] {'x'}, dimensions={0} | all-to-all | bytes 1048576 | tf_op jit(solution)/shard_map/all_to_all | solution.py:70
  20.6 1.1 copy.186
  21.7 2.2 %collective-permute-start.1 = (bf16[4096,128]{1,0:T(8,128)(2,1)S(1)}, bf16[4096,128]{1,0:T(8,128)(2,1)}, u32[]{:S(2)}, u32[]{:S(2)}) collective-permute-start(bf16[4096,128]{1,0:T(8,128)(2,1)S(1)} %bitcast.145), channel_id=1, source_target_pairs={{0,8},{8,16},{16,24},{24,0},{1,9},{9,17},{17,25},{25,1},{2,10},{10... | collective-permute-start | bytes 3145736 | tf_op jit(solution)/shard_map/ppermute | solution.py:38
  23.9 4.3 %collective-permute-start = (bf16[4096,128]{1,0:T(8,128)(2,1)S(1)}, bf16[4096,128]{1,0:T(8,128)(2,1)}, u32[]{:S(2)}, u32[]{:S(2)}) collective-permute-start(bf16[4096,128]{1,0:T(8,128)(2,1)S(1)} %bitcast.146), channel_id=1, source_target_pairs={{0,24},{8,0},{16,8},{24,16},{1,25},{9,1},{17,9},{25,17},{2,26},{10... | collective-permute-start | bytes 3145736 | tf_op jit(solution)/shard_map/ppermute | solution.py:38
  28.3 2.0 copy.189
  30.3 3.5 %all-to-all-start.1 = ((bf16[4,128,512]{1,2,0:T(8,128)(2,1)}), bf16[4,128,512]{1,2,0:T(8,128)(2,1)S(1)}, u32[]{:S(2)}, u32[]{:S(2)}) async-start(bf16[4,128,512]{1,2,0:T(8,128)(2,1)} %bitcast.22), calls=%async_computation.1 | async-start | bytes 1048576 | tf_op jit(solution)/shard_map/all_to_all | solution.py:73
  34.4 1.1 copy.192
  35.7 1.3 copy.184
  37.1 3.7 %fusion = f32[384,128]{1,0:T(8,128)S(1)} fusion(bf16[4096,128]{1,0:T(8,128)(2,1)} %bitcast.152, s32[384]{0:T(512)S(1)} %dynamic-slice_reduce_fusion, s32[4096]{0:T(1024)S(1)} %bitcast.166), kind=kOutput, calls=%fused_computation.3 | convolution fusion | flops 404226048 | bytes 1263104 | tf_op jit(solution)/shard_map/dot_general | solution.py:33
  40.8 3.9 %collective-permute-done = bf16[4096,128]{1,0:T(8,128)(2,1)} collective-permute-done((bf16[4096,128]{1,0:T(8,128)(2,1)S(1)}, bf16[4096,128]{1,0:T(8,128)(2,1)}, u32[]{:S(2)}, u32[]{:S(2)}) %collective-permute-start) | collective-permute-done | bytes 1048608 | tf_op jit(solution)/shard_map/ppermute | solution.py:38
  44.7 1.1 slice.91
  45.8 5.4 %collective-permute-start.3 = (bf16[2048,128]{1,0:T(8,128)(2,1)S(1)}, bf16[2048,128]{1,0:T(8,128)(2,1)}, u32[]{:S(2)}, u32[]{:S(2)}) collective-permute-start(bf16[2048,128]{1,0:T(8,128)(2,1)S(1)} %slice.91), channel_id=1, source_target_pairs={{0,24},{8,0},{16,8},{24,16},{1,25},{9,1},{17,9},{25,17},{2,26},{10... | collective-permute-start | bytes 1572872 | tf_op jit(solution)/shard_map/ppermute | solution.py:38
  51.2 1.1 slice.90
  52.3 2.1 collective-permute-start.2
  54.4 31.0 %all-gather.2.cloned.1.call-done = bf16[4096,512]{0,1:T(8,128)(2,1)} async-done(((bf16[512,512]{0,1:T(8,128)(2,1)}), bf16[4096,512]{0,1:T(8,128)(2,1)}) %all-gather.2.cloned.1.call-update) | async-done | bytes 4194320 | tf_op jit(solution)/shard_map/all_gather | solution.py:71
  85.5 4.1 %convolution_bitcast_fusion.3 = f32[1,16,8,4,128]{4,2,3,1,0:T(8,128)S(1)} fusion(bf16[4,128,4096,1]{2,1,0,3:T(8,128)(2,1)} %bitcast.138, bf16[128,4096]{1,0:T(8,128)(2,1)} %copy.184), kind=kOutput, calls=%fused_computation.26 | convolution fusion | flops 536870912 | bytes 5505024 | tf_op jit(solution)/shard_map/dot_general | solution.py:33
  89.6 2.7 %convolution_bitcast_fusion = f32[1,16,8,4,128]{4,2,3,1,0:T(8,128)S(1)} fusion(bf16[4096,128]{1,0:T(8,128)(2,1)} %collective-permute-done.1, bf16[4096,512]{0,1:T(8,128)(2,1)S(1)} %copy-done), kind=kOutput, calls=%fused_computation.23 | convolution fusion | flops 536870912 | bytes 5505024 | tf_op jit(solution)/shard_map/dot_general | solution.py:33
  92.4 2.7 %convolution_bitcast_fusion.2 = f32[1,16,8,4,128]{4,2,3,1,0:T(8,128)S(1)} fusion(bf16[4096,128]{1,0:T(8,128)(2,1)} %collective-permute-done, bf16[4096,512]{0,1:T(8,128)(2,1)S(1)} %copy-done), kind=kOutput, calls=%fused_computation.25 | convolution fusion | flops 536870912 | bytes 5505024 | tf_op jit(solution)/shard_map/dot_general | solution.py:33
  95.1 2.6 %convolution_bitcast_fusion.1 = f32[1,16,8,4,128]{4,2,3,1,0:T(8,128)S(1)} fusion(bf16[4096,512]{0,1:T(8,128)(2,1)S(1)} %copy-done, bf16[2048,128]{1,0:T(8,128)(2,1)} %collective-permute-done.3, bf16[2048,128]{1,0:T(8,128)(2,1)S(1)} %collective-permute-done.2), kind=kOutput, calls=%fused_computation.24 | convolution fusion | flops 538968064 | bytes 5505024 | tf_op jit(solution)/shard_map/dot_general | solution.py:33
  97.9 2.5 %fusion.5 = f32[384,512]{1,0:T(8,128)S(1)} fusion(bf16[4096,512]{0,1:T(8,128)(2,1)S(1)} %copy-done, s32[384]{0:T(512)S(1)} %eq.126, s32[4096]{0:T(1024)S(1)} %bitcast.165), kind=kOutput, calls=%fused_computation.9 | convolution fusion | flops 1613758464 | bytes 4998656 | tf_op jit(solution)/shard_map/dot_general | solution.py:33
  100.6 4.8 %fusion.4 = f32[384,512]{1,0:T(8,128)S(1)} fusion(bf16[4096,512]{0,1:T(8,128)(2,1)} %all-gather.2.cloned.1.call-done, s32[384]{0:T(512)S(1)} %eq.120, s32[4096]{0:T(1024)S(1)} %bitcast.164), kind=kOutput, calls=%fused_computation.8 | convolution fusion | flops 1613758464 | bytes 4998656 | tf_op jit(solution)/shard_map/dot_general | solution.py:33
  105.7 2.5 %fusion.3 = f32[384,512]{1,0:T(8,128)S(1)} fusion(bf16[4096,512]{0,1:T(8,128)(2,1)S(1)} %copy-done.1, s32[384]{0:T(512)S(1)} %eq.114, s32[4096]{0:T(1024)S(1)} %bitcast.163), kind=kOutput, calls=%fused_computation.7 | convolution fusion | flops 1613758464 | bytes 4998656 | tf_op jit(solution)/shard_map/dot_general | solution.py:33
  108.2 0.3 fusion.40
  108.5 2.7 %fusion.2 = f32[384,512]{1,0:T(8,128)S(1)} fusion(bf16[4096,512]{0,1:T(8,128)(2,1)S(1)} %copy-done.1, s32[384]{0:T(512)S(1)} %eq.103, s32[4096]{0:T(1024)S(1)} %bitcast.162), kind=kOutput, calls=%fused_computation.6 | convolution fusion | flops 1613758464 | bytes 4998656 | tf_op jit(solution)/shard_map/dot_general | solution.py:33
  111.5 0.3 fusion.17
  111.7 0.3 fusion.19
  112.0 0.3 fusion.21
  112.3 0.3 fusion.23
  112.8 2.7 %collective-permute-start.4 = (f32[8,224,128]{2,1,0:T(8,128)S(1)}, f32[8,224,128]{2,1,0:T(8,128)S(1)}, u32[]{:S(2)}, u32[]{:S(2)}) collective-permute-start(f32[8,224,128]{2,1,0:T(8,128)S(1)} %select_bitcast_fusion), channel_id=1, source_target_pairs={{0,32},{32,0},{1,33},{33,1},{2,34},{34,2},{3,35},{35,3},{4,36},{36... | collective-permute-start | bytes 2752520 | tf_op jit(solution)/shard_map/ppermute | solution.py:38
  115.5 2.1 collective-permute-done.4
  117.6 1.1 fusion.30
  118.7 6.5 %all-to-all-start.2 = ((f32[8,224,128]{2,1,0:T(8,128)}), f32[8,224,128]{2,1,0:T(8,128)S(1)}, u32[]{:S(2)}, u32[]{:S(2)}) async-start(f32[8,224,128]{2,1,0:T(8,128)} %fusion.30), calls=%async_computation.2 | async-start | bytes 1835008 | tf_op jit(solution)/shard_map/all_to_all | solution.py:115
  125.2 26.4 %all-to-all-done.2 = f32[8,224,128]{2,1,0:T(8,128)S(1)} async-done(((f32[8,224,128]{2,1,0:T(8,128)}), f32[8,224,128]{2,1,0:T(8,128)S(1)}, u32[]{:S(2)}, u32[]{:S(2)}) %all-to-all-start.2) | async-done | bytes 917536 | tf_op jit(solution)/shard_map/all_to_all | solution.py:115
  151.6 0.7 copy.200
  152.3 6.6 %all-to-all-start.4 = ((f32[32,3,128]{2,1,0:T(4,128)}), f32[32,3,128]{2,1,0:T(4,128)S(1)}, u32[]{:S(2)}, u32[]{:S(2)}) async-start(f32[32,3,128]{2,1,0:T(4,128)} %copy.200), calls=%async_computation.4 | async-start | bytes 131072 | tf_op jit(solution)/shard_map/all_to_all | solution.py:126
  159.0 0.7 fusion.45
  159.6 8.2 %all-to-all-done.4 = f32[32,3,128]{2,1,0:T(4,128)S(1)} async-done(((f32[32,3,128]{2,1,0:T(4,128)}), f32[32,3,128]{2,1,0:T(4,128)S(1)}, u32[]{:S(2)}, u32[]{:S(2)}) %all-to-all-start.4) | async-done | bytes 49184 | tf_op jit(solution)/shard_map/all_to_all | solution.py:126
  167.8 3.3 %all-to-all-start.3 = ((f32[4,32,128]{2,1,0:T(8,128)}), f32[4,32,128]{2,1,0:T(8,128)S(1)}, u32[]{:S(2)}, u32[]{:S(2)}) async-start(f32[4,32,128]{2,1,0:T(8,128)} %fusion.45), calls=%async_computation.3 | async-start | bytes 131072 | tf_op jit(solution)/shard_map/all_to_all | solution.py:122
  171.1 4.4 %all-to-all-done.3 = f32[4,32,128]{2,1,0:T(8,128)S(1)} async-done(((f32[4,32,128]{2,1,0:T(8,128)}), f32[4,32,128]{2,1,0:T(8,128)S(1)}, u32[]{:S(2)}, u32[]{:S(2)}) %all-to-all-start.3) | async-done | bytes 65568 | tf_op jit(solution)/shard_map/all_to_all | solution.py:122
  175.6 18.7 %all_to_all.31 = f32[8,152,128]{2,1,0:T(8,128)S(1)} all-to-all(f32[8,152,128]{2,1,0:T(8,128)S(1)} %broadcast_in_dim.34), channel_id=1, replica_groups=mesh['y'=8,'core'=2,'x'=4,'z'=8] {'y'}, dimensions={0} | all-to-all | bytes 1245184 | tf_op jit(solution)/shard_map/all_to_all | solution.py:132
  194.3 6.2 %collective-permute-start.5 = (f32[8,152,128]{2,1,0:T(8,128)S(1)}, f32[8,152,128]{2,1,0:T(8,128)S(1)}, u32[]{:S(2)}, u32[]{:S(2)}) collective-permute-start(f32[8,152,128]{2,1,0:T(8,128)S(1)} %all_to_all.31), channel_id=1, source_target_pairs={{0,32},{32,0},{1,33},{33,1},{2,34},{34,2},{3,35},{35,3},{4,36},{36... | collective-permute-start | bytes 1867784 | tf_op jit(solution)/shard_map/ppermute | solution.py:38
  200.8 1.4 collective-permute-done.5
  202.4 1.1 slice_bitcast_fusion
  203.6 0.5 copy_select_fusion
  204.0 0.8 copy.210
  204.8 0.8 copy.211
  205.7 0.8 copy.212
  (59 shorter events, 2.9 us)
Async XLA Ops:
  7.2 14.5 %copy-start.2 = (bf16[2,2048,128]{2,1,0:T(8,128)(2,1)S(1)}, bf16[2,2048,128]{2,1,0:T(8,128)(2,1)}, u32[]{:S(2)}) copy-start(bf16[2,2048,128]{2,1,0:T(8,128)(2,1)} %param.9) | copy-start | bytes 3145732
  7.2 78.3 %all-gather.2.cloned.1.call-start = ((), (), s32[]{:S(2)}) async-start(), calls=%async_computation.6 | async-start | bytes 4718592 | tf_op jit(solution)/shard_map/all_gather | solution.py:71
  8.7 25.1 %copy-start.4 = (s32[32,4,12]{0,1,2:T(4,128)S(1)}, s32[32,4,12]{0,1,2:T(4,128)}, u32[]{:S(2)}) copy-start(s32[32,4,12]{0,1,2:T(4,128)} %param.14) | copy-start | bytes 18436
  8.7 25.2 %copy-start.8 = (s32[2,2048,4]{1,2,0:T(4,128)S(1)}, s32[2,2048,4]{1,2,0:T(4,128)}, u32[]{:S(2)}) copy-start(s32[2,2048,4]{1,2,0:T(4,128)} %param.13) | copy-start | bytes 196612
  8.8 25.6 %copy-start.3 = (bf16[2,2048,128]{2,1,0:T(8,128)(2,1)S(1)}, bf16[2,2048,128]{2,1,0:T(8,128)(2,1)}, u32[]{:S(2)}) copy-start(bf16[2,2048,128]{2,1,0:T(8,128)(2,1)} %param.10) | copy-start | bytes 3145732
  21.7 29.5 %collective-permute-start.1 = (bf16[4096,128]{1,0:T(8,128)(2,1)S(1)}, bf16[4096,128]{1,0:T(8,128)(2,1)}, u32[]{:S(2)}, u32[]{:S(2)}) collective-permute-start(bf16[4096,128]{1,0:T(8,128)(2,1)S(1)} %bitcast.145), channel_id=1, source_target_pairs={{0,8},{8,16},{16,24},{24,0},{1,9},{9,17},{17,25},{25,1},{2,10},{10... | collective-permute-start | bytes 3145736 | tf_op jit(solution)/shard_map/ppermute | solution.py:38
  23.9 20.8 %collective-permute-start = (bf16[4096,128]{1,0:T(8,128)(2,1)S(1)}, bf16[4096,128]{1,0:T(8,128)(2,1)}, u32[]{:S(2)}, u32[]{:S(2)}) collective-permute-start(bf16[4096,128]{1,0:T(8,128)(2,1)S(1)} %bitcast.146), channel_id=1, source_target_pairs={{0,24},{8,0},{16,8},{24,16},{1,25},{9,1},{17,9},{25,17},{2,26},{10... | collective-permute-start | bytes 3145736 | tf_op jit(solution)/shard_map/ppermute | solution.py:38
  30.3 70.1 %all-to-all-start.1 = ((bf16[4,128,512]{1,2,0:T(8,128)(2,1)}), bf16[4,128,512]{1,2,0:T(8,128)(2,1)S(1)}, u32[]{:S(2)}, u32[]{:S(2)}) async-start(bf16[4,128,512]{1,2,0:T(8,128)(2,1)} %bitcast.22), calls=%async_computation.1 | async-start | bytes 1048576 | tf_op jit(solution)/shard_map/all_to_all | solution.py:73
  45.8 49.3 %collective-permute-start.3 = (bf16[2048,128]{1,0:T(8,128)(2,1)S(1)}, bf16[2048,128]{1,0:T(8,128)(2,1)}, u32[]{:S(2)}, u32[]{:S(2)}) collective-permute-start(bf16[2048,128]{1,0:T(8,128)(2,1)S(1)} %slice.91), channel_id=1, source_target_pairs={{0,24},{8,0},{16,8},{24,16},{1,25},{9,1},{17,9},{25,17},{2,26},{10... | collective-permute-start | bytes 1572872 | tf_op jit(solution)/shard_map/ppermute | solution.py:38
  52.3 42.8 %collective-permute-start.2 = (bf16[2048,128]{1,0:T(8,128)(2,1)S(1)}, bf16[2048,128]{1,0:T(8,128)(2,1)S(1)}, u32[]{:S(2)}, u32[]{:S(2)}) collective-permute-start(bf16[2048,128]{1,0:T(8,128)(2,1)S(1)} %slice.90), channel_id=1, source_target_pairs={{0,8},{8,16},{16,24},{24,0},{1,9},{9,17},{17,25},{25,1},{2,10},{10... | collective-permute-start | bytes 1572872 | tf_op jit(solution)/shard_map/ppermute | solution.py:38
  85.5 4.2 %copy-start = (bf16[4096,512]{0,1:T(8,128)(2,1)S(1)}, bf16[4096,512]{0,1:T(8,128)(2,1)}, u32[]{:S(2)}) copy-start(bf16[4096,512]{0,1:T(8,128)(2,1)} %all-gather.2.cloned.1.call-done) | copy-start | bytes 12582916
  100.6 5.1 %copy-start.1 = (bf16[4096,512]{0,1:T(8,128)(2,1)S(1)}, bf16[4096,512]{0,1:T(8,128)(2,1)}, u32[]{:S(2)}) copy-start(bf16[4096,512]{0,1:T(8,128)(2,1)} %all-gather.2.cloned.1.call-done) | copy-start | bytes 12582916
  112.8 4.8 %collective-permute-start.4 = (f32[8,224,128]{2,1,0:T(8,128)S(1)}, f32[8,224,128]{2,1,0:T(8,128)S(1)}, u32[]{:S(2)}, u32[]{:S(2)}) collective-permute-start(f32[8,224,128]{2,1,0:T(8,128)S(1)} %select_bitcast_fusion), channel_id=1, source_target_pairs={{0,32},{32,0},{1,33},{33,1},{2,34},{34,2},{3,35},{35,3},{4,36},{36... | collective-permute-start | bytes 2752520 | tf_op jit(solution)/shard_map/ppermute | solution.py:38
  118.7 32.9 %all-to-all-start.2 = ((f32[8,224,128]{2,1,0:T(8,128)}), f32[8,224,128]{2,1,0:T(8,128)S(1)}, u32[]{:S(2)}, u32[]{:S(2)}) async-start(f32[8,224,128]{2,1,0:T(8,128)} %fusion.30), calls=%async_computation.2 | async-start | bytes 1835008 | tf_op jit(solution)/shard_map/all_to_all | solution.py:115
  152.3 15.5 %all-to-all-start.4 = ((f32[32,3,128]{2,1,0:T(4,128)}), f32[32,3,128]{2,1,0:T(4,128)S(1)}, u32[]{:S(2)}, u32[]{:S(2)}) async-start(f32[32,3,128]{2,1,0:T(4,128)} %copy.200), calls=%async_computation.4 | async-start | bytes 131072 | tf_op jit(solution)/shard_map/all_to_all | solution.py:126
  167.8 7.7 %all-to-all-start.3 = ((f32[4,32,128]{2,1,0:T(8,128)}), f32[4,32,128]{2,1,0:T(8,128)S(1)}, u32[]{:S(2)}, u32[]{:S(2)}) async-start(f32[4,32,128]{2,1,0:T(8,128)} %fusion.45), calls=%async_computation.3 | async-start | bytes 131072 | tf_op jit(solution)/shard_map/all_to_all | solution.py:122
  194.3 9.2 %copy-start.5 = (f32[1,4,12,1024]{3,1,2,0:T(4,128)S(1)}, f32[1,4,12,1024]{3,1,2,0:T(4,128)}, u32[]{:S(2)}) copy-start(f32[1,4,12,1024]{3,1,2,0:T(4,128)} %param.17) | copy-start | bytes 589828
  194.3 9.2 %copy-start.6 = (f32[1,4,12,1024]{3,1,2,0:T(4,128)S(1)}, f32[1,4,12,1024]{3,1,2,0:T(4,128)}, u32[]{:S(2)}) copy-start(f32[1,4,12,1024]{3,1,2,0:T(4,128)} %param.16) | copy-start | bytes 589828
  194.3 9.2 %copy-start.7 = (f32[1,4,12,1024]{3,1,2,0:T(4,128)S(1)}, f32[1,4,12,1024]{3,1,2,0:T(4,128)}, u32[]{:S(2)}) copy-start(f32[1,4,12,1024]{3,1,2,0:T(4,128)} %param.15) | copy-start | bytes 589828
  194.3 7.9 %collective-permute-start.5 = (f32[8,152,128]{2,1,0:T(8,128)S(1)}, f32[8,152,128]{2,1,0:T(8,128)S(1)}, u32[]{:S(2)}, u32[]{:S(2)}) collective-permute-start(f32[8,152,128]{2,1,0:T(8,128)S(1)} %all_to_all.31), channel_id=1, source_target_pairs={{0,32},{32,0},{1,33},{33,1},{2,34},{34,2},{3,35},{35,3},{4,36},{36... | collective-permute-start | bytes 1867784 | tf_op jit(solution)/shard_map/ppermute | solution.py:38
Sparse Core Ops, SparseCore 0:
  21.8 63.6 all-gather.1
